TPU v7x, 256 devices: a whole 4x4x8 slice. The times are simulated.
256 devices in a mesh: tm: 8 (over y_hi, x), stream: 32 (over y_lo, z, core).
Axes of the slice: x: 4, y: 4 (y_hi: 2, y_lo: 2; y = y_hi * 2 + y_lo), z: 8, core: 2. Of those that a mesh axis runs over, the one named last changes fastest.
Arguments:
- tokens: bfloat16 [32, 1024, 768], P('stream', 'tm'), may hold values from -6 to 6
- cotangent: bfloat16 [32, 1024, 768], P('stream', 'tm'), may hold values from -6 to 6
- decay: float32 [32, 1024, 24], P('stream', 'tm'), may hold values from 0.4 to 1, as said below
- in_w: bfloat16 [768, 3328], P('stream'), may hold values from -0.21875 to 0.21875
- out_w: bfloat16 [1536, 768], P('stream'), may hold values from -0.15625 to 0.15625
- conv_w: float32 [4, 1792], replicated, may hold values from -3 to 3
- dskip: float32 [24], replicated, may hold values from 0.5 to 2
- norm_w: float32 [1536], replicated, may hold values from 0.1 to 1.9
Outputs:
- out: bfloat16 [32, 1024, 768], P('stream', 'tm')
- grad_tokens: bfloat16 [32, 1024, 768], P('stream', 'tm')
- grad_out_t: float32 [768, 1536], P(('tm', 'stream'))
Inputs may be any that keep to these rules, and one draw needn't show every extreme that they name: decay lies strictly between 0 and 1.
All inputs are finite; a program needn't handle non-finite values.
Results may differ from a plain program's by a relative error of at most 0.015.
Values may be sent and summed in bfloat16 or wider, within the bound.
No kernel may reach another device: no remote copies, remote signals or barrier semaphores. Data moves between devices by JAX's collectives and lax.ppermute only.
A program may use at most 128 MiB of HBM per device.

v0:
```python
import jax
import jax.numpy as jnp
from jax import lax
from jax.sharding import PartitionSpec as P

block_len = 128
working = lax.Precision.HIGH


def shifted(value, axis, steps):
    count = lax.axis_size(axis)
    initial, last = (max(0, -steps), min(count, count - steps))
    return lax.ppermute(value, axis, [(source, source + steps) for source in range(initial, last)])


def entering(value, axis, join, neutral):
    count, mine = (lax.axis_size(axis), lax.axis_index(axis))
    pieces = jax.tree.map(lambda part: lax.all_gather(part, axis), value)
    running = jax.tree.map(
        lambda part, zero: jnp.full_like(part, 0) + jnp.asarray(zero, part.dtype), value, neutral
    )

    def step(position, running):
        longer = join(running, jax.tree.map(lambda part: part[position], pieces))
        return jax.tree.map(lambda new, old: jnp.where(position < mine, new, old), longer, running)

    return lax.fori_loop(0, count - 1, step, running)


def carried_in(shard, axis, join, neutral):
    count = lax.axis_size(axis)
    place = lax.axis_index(axis)
    ahead = count - 1 - place
    gathered = jax.tree.map(
        lambda a, kind: lax.all_gather(a.astype(kind), axis),
        shard,
        jax.tree.map(lambda a: jnp.bfloat16 if a.dtype == jnp.float32 else a.dtype, shard),
    )
    state = jax.tree.map(lambda a, e: jnp.zeros_like(a) + jnp.asarray(e, a.dtype), shard, neutral)

    def one(step, state):
        source = count - 1 - step
        return join(
            state,
            jax.tree.map(
                lambda a, own: lax.dynamic_index_in_dim(a, source, 0, False).astype(own.dtype),
                gathered,
                shard,
            ),
        )

    return lax.fori_loop(0, ahead, one, state)


def conv_apply(extended, conv_weight):
    conv_taps = conv_weight.shape[0]
    row_count = extended.shape[0] - conv_taps + 1
    result = jnp.zeros((row_count, extended.shape[1]), jnp.float32)
    for offset in range(conv_taps):
        result = result + conv_weight[offset] * extended[offset : offset + row_count]
    return result


def block_ssm(carry_state, x_block, b_block, c_block, decay_log):
    cumulative = jnp.cumsum(decay_log, axis=0)
    carried = jnp.exp(cumulative)[:, :, None] * jnp.einsum(
        "tn,hpn->thp", c_block, carry_state, precision=working
    )
    scores = jnp.einsum("tn,sn->ts", c_block, b_block, precision=working)
    later_idx = lax.broadcasted_iota(jnp.int32, scores.shape, 0)
    earlier_idx = lax.broadcasted_iota(jnp.int32, scores.shape, 1)
    causal = (later_idx >= earlier_idx)[:, :, None]
    log_gap = cumulative[:, None, :] - cumulative[None, :, :]
    weight = jnp.where(causal, jnp.exp(jnp.where(causal, log_gap, 0.0)), 0.0) * scores[:, :, None]
    inside = jnp.einsum("tsh,shp->thp", weight, x_block, precision=working)
    fade_out = jnp.exp(cumulative[-1][None, :] - cumulative)
    added = jnp.einsum("shp,sn->hpn", fade_out[:, :, None] * x_block, b_block, precision=working)
    carry_state = jnp.exp(cumulative[-1])[:, None, None] * carry_state + added
    return (carried + inside, carry_state)


def local_scan(conv_out, decay_log, skip_gain, head_count, state_width):
    row_count = conv_out.shape[0]
    inner_width = conv_out.shape[1] - 2 * state_width
    head_dim = inner_width // head_count
    block_rows = min(block_len, row_count)
    blocks = row_count // block_rows
    x_all = conv_out[:, :inner_width].reshape(blocks, block_rows, head_count, head_dim)
    b_all = conv_out[:, inner_width : inner_width + state_width].reshape(
        blocks, block_rows, state_width
    )
    c_all = conv_out[:, inner_width + state_width :].reshape(blocks, block_rows, state_width)
    d_all = decay_log.reshape(blocks, block_rows, head_count)

    def advance(carry_state, pieces):
        outputs, carry_state = block_ssm(carry_state, pieces[0], pieces[1], pieces[2], pieces[3])
        return (carry_state, outputs)

    start_state = jnp.zeros((head_count, head_dim, state_width), jnp.float32)
    final_state, results = lax.scan(advance, start_state, (x_all, b_all, c_all, d_all))
    x_heads = conv_out[:, :inner_width].reshape(row_count, head_count, head_dim)
    outputs = results.reshape(row_count, head_count, head_dim) + skip_gain[None, :, None] * x_heads
    return (outputs.reshape(row_count, inner_width), final_state)


def gate_norm(ssm_out, gate_in, norm_gain):
    gated = ssm_out * jax.nn.silu(gate_in)
    factor = lax.rsqrt(jnp.mean(gated * gated, axis=-1, keepdims=True) + 1e-05)
    return gated * factor * norm_gain


def combine_carry(earlier, later):
    return (earlier[0] * later[0], later[0][:, None, None] * earlier[1] + later[1])


def shards(tokens, cotangent, decay, in_w, out_w, conv_w, dskip, norm_w):
    inputs = tokens[0]
    grad_out = cotangent[0]
    decay_log = jnp.log(decay[0])
    row_count = inputs.shape[0]
    head_count = dskip.shape[0]
    full_in, full_out = (
        lax.all_gather(in_w, "stream", axis=0, tiled=True),
        lax.all_gather(out_w, "stream", axis=0, tiled=True),
    )
    inner_width = full_out.shape[0]
    proj_width = full_in.shape[1]
    state_width = (proj_width - 2 * inner_width) // 2
    head_dim = inner_width // head_count
    conv_taps = conv_w.shape[0]
    projected = jnp.dot(inputs, full_in, preferred_element_type=jnp.float32).astype(jnp.bfloat16)
    gate_in = projected[:, :inner_width].astype(jnp.float32)
    mix_in = projected[:, inner_width:]
    rim_rows = shifted(mix_in[row_count - conv_taps + 1 :], "tm", 1)
    extended = jnp.concatenate([rim_rows, mix_in], axis=0).astype(jnp.float32)

    def conv_part(values):
        return conv_apply(values, conv_w)

    pre_act, conv_back = jax.vjp(conv_part, extended)
    conv_low = jax.nn.silu(pre_act).astype(jnp.bfloat16)
    conv_out = lax.optimization_barrier(conv_low).astype(jnp.float32)

    def scan_part(values):
        return local_scan(values, decay_log, dskip, head_count, state_width)

    (ssm_local, state_local), ssm_back = jax.vjp(scan_part, conv_out)
    cumulative = jnp.cumsum(decay_log, axis=0)
    decay_total = jnp.exp(cumulative[-1])
    identity = (jnp.ones_like(decay_total), jnp.zeros_like(state_local))
    state_in = entering((decay_total, state_local), "tm", combine_carry, identity)[1]
    b_vecs = conv_out[:, inner_width : inner_width + state_width]
    c_vecs = conv_out[:, inner_width + state_width :]
    x_heads = conv_out[:, :inner_width].reshape(row_count, head_count, head_dim)
    growth = jnp.exp(cumulative)
    carried = growth[:, :, None] * jnp.einsum("tn,hpn->thp", c_vecs, state_in, precision=working)
    ssm_out = ssm_local + carried.reshape(row_count, inner_width)

    def norm_part(ssm_values, gate_values):
        return gate_norm(ssm_values, gate_values, norm_w)

    normed, norm_back = jax.vjp(norm_part, ssm_out, gate_in)
    normed_low = normed.astype(jnp.bfloat16)
    result = jnp.dot(normed_low, full_out, preferred_element_type=jnp.float32).astype(jnp.bfloat16)
    grad_normed = jnp.einsum("td,ed->te", grad_out, full_out, preferred_element_type=jnp.float32)
    grad_ssm, grad_gate = norm_back(grad_normed)
    grad_heads = grad_ssm.reshape(row_count, head_count, head_dim)
    weighted = growth[:, :, None] * grad_heads
    adjoint_local = jnp.einsum("thp,tn->hpn", weighted, c_vecs, precision=working)
    adjoint_in = carried_in((decay_total, adjoint_local), "tm", combine_carry, identity)[1]
    (grad_local,) = ssm_back((grad_ssm, jnp.zeros_like(state_local)))
    fade_out = jnp.exp(cumulative[-1][None, :] - cumulative)
    grad_x = fade_out[:, :, None] * jnp.einsum("hpn,tn->thp", adjoint_in, b_vecs, precision=working)
    grad_b = jnp.einsum(
        "thp,hpn->tn", fade_out[:, :, None] * x_heads, adjoint_in, precision=working
    )
    grad_c = jnp.einsum("thp,hpn->tn", weighted, state_in, precision=working)
    grad_conv = grad_local + jnp.concatenate(
        [grad_x.reshape(row_count, inner_width), grad_b, grad_c], axis=1
    )
    sigmoid_pre = jax.nn.sigmoid(pre_act)
    (grad_ext,) = conv_back(grad_conv * sigmoid_pre * (1.0 + pre_act * (1.0 - sigmoid_pre)))
    incoming = shifted(grad_ext[: conv_taps - 1], "tm", -1)
    grad_mix = grad_ext[conv_taps - 1 :] + jnp.pad(
        incoming, ((row_count - conv_taps + 1, 0), (0, 0))
    )
    grad_proj = jnp.concatenate([grad_gate, grad_mix], axis=1).astype(jnp.bfloat16)
    grad_tokens = jnp.einsum(
        "tj,dj->td", grad_proj, full_in, preferred_element_type=jnp.float32
    ).astype(jnp.bfloat16)
    n_time = lax.axis_size("tm")
    n_stream = lax.axis_size("stream")
    grad_scale = (n_time * n_stream * row_count) ** (-0.5)
    summed = lax.psum_scatter(
        jnp.einsum("td,te->de", grad_out, normed_low, preferred_element_type=jnp.float32),
        ("tm", "stream"),
        scatter_dimension=0,
        tiled=True,
    )
    return (result[None], grad_tokens[None], summed * grad_scale)


def solution(mesh):
    in_specs = (
        P("stream", "tm", None),
        P("stream", "tm", None),
        P("stream", "tm", None),
        P("stream", None),
        P("stream", None),
        P(),
        P(),
        P(),
    )
    out_specs = (P("stream", "tm", None), P("stream", "tm", None), P(("tm", "stream"), None))
    return jax.shard_map(shards, mesh=mesh, in_specs=in_specs, out_specs=out_specs, check_vma=False)
```

profile of v0, /device:TPU:32, one launch (start us, length us, event | category | flops | bytes accessed | tf_op | source)
XLA Modules:
  0.0 630.5 jit_solution(17365361491446200378)
XLA Ops:
  9.0 70.2 %all-gather.9.cloned.1.call-done = bf16[768,3328]{1,0:T(8,128)(2,1)} async-done(((bf16[24,3328]{1,0:T(8,128)(2,1)}), bf16[768,3328]{1,0:T(8,128)(2,1)}) %all-gather.9.cloned.1.call-update) | async-done | bytes 5111824 | tf_op jit(solution)/shard_map/all_gather | solution.py:123
  79.2 3.4 convolution_convert_fusion
  82.7 3.4 collective-permute-start
  87.5 1.5 multiply_convert_fusion
  91.8 24.1 %all-gather.2 = f32[8,1,24]{2,1,0:T(1,128)S(1)} all-gather(f32[1,1,24]{2,1,0:T(1,128)S(1)} %get-tuple-element.413), channel_id=1, replica_groups=mesh['tm'=8,'stream'=32] {'tm'}, dimensions={0}, use_global_device_ids=true | all-gather | bytes 864 | tf_op jit(solution)/shard_map/all_gather | solution.py:18
  117.0 2.3 fusion.7
  120.8 67.1 %all-gather.13.cloned.1.call-done = f32[192,64,128]{2,1,0:T(8,128)} async-done(((f32[24,64,128]{2,1,0:T(8,128)}), f32[192,64,128]{2,1,0:T(8,128)}) %all-gather.13.cloned.1.call-update) | async-done | bytes 6291472 | tf_op jit(solution)/shard_map/all_gather | solution.py:18
  187.9 9.4 %while.21 = (s32[]{:T(128)}, f32[24,64,128]{2,1,0:T(8,128)S(1)}, s32[]{:T(128)}, f32[8,24]{1,0:T(8,128)S(1)}, f32[8,24,64,128]{3,2,1,0:T(8,128)}, /*index=5*/s32[]{:T(128)}, s32[]{:T(128)}) while((s32[]{:T(128)}, f32[24,64,128]{2,1,0:T(8,128)S(1)}, s32[]{:T(128)}, f32[8,24]{1,0:T(8,128)S(1)}, f32[8,24,64,128]{3,2,1,0:T(8,128)}, ...), condition=%wide.region_2.3_spmd.clone, body=%wide.region_1.2_spmd.clone.sunk | while | flops 786436 | bytes 2359697 | solution.py:27
  189.2 1.3 fusion.109
  198.8 52.8 %all-gather.11.cloned.1.call-done = bf16[1536,768]{1,0:T(8,128)(2,1)} async-done(((bf16[48,768]{1,0:T(8,128)(2,1)}), bf16[1536,768]{1,0:T(8,128)(2,1)}) %all-gather.11.cloned.1.call-update) | async-done | bytes 2359312 | tf_op jit(solution)/shard_map/all_gather | solution.py:124
  251.7 4.0 multiply_reduce_fusion
  255.7 3.0 convolution_bitcast_fusion
  258.8 3.5 broadcast_multiply_fusion.4
  262.6 1.9 convolution_convert_fusion.1
  264.5 23.2 %all-gather.3 = bf16[8,1,24]{2,1,0:T(2,128)(2,1)S(1)} all-gather(bf16[1,1,24]{2,1,0:T(2,128)(2,1)S(1)} %get-tuple-element.411), channel_id=1, replica_groups=mesh['tm'=8,'stream'=32] {'tm'}, dimensions={0}, use_global_device_ids=true | all-gather | bytes 432 | tf_op jit(solution)/shard_map/all_gather | solution.py:35
  288.7 2.3 copy.57
  292.9 2.1 fusion.14
  294.9 2.3 copy.59
  297.2 2.1 mul.434
  299.4 1.4 copy.58
  302.4 1.3 fusion.1
  303.7 1.6 convolution_add_fusion.1
  305.3 1.5 convolution_add_fusion.2
  308.1 221.1 %all-reduce.12.cloned.1.call-done = f32[768,1536]{0,1:T(8,128)} async-done(((f32[768,1536]{0,1:T(8,128)}), f32[768,1536]{0,1:T(8,128)}) %all-reduce.12.cloned.1.call-update) | async-done | bytes 4718608
  529.2 1.7 dynamic-slice_multiply_fusion
  531.8 68.9 %all-gather.15.cloned.1.call-done = bf16[192,64,128]{2,1,0:T(8,128)(2,1)} async-done(((bf16[24,64,128]{2,1,0:T(8,128)(2,1)}), bf16[192,64,128]{2,1,0:T(8,128)(2,1)}) %all-gather.15.cloned.1.call-update) | async-done | bytes 3145744 | tf_op jit(solution)/shard_map/all_gather | solution.py:35
  600.8 8.7 %while.20 = (s32[]{:T(128)}, f32[24,64,128]{2,1,0:T(8,128)S(1)}, s32[]{:T(128)}, bf16[8,24]{1,0:T(8,128)(2,1)S(1)}, bf16[8,24,64,128]{3,2,1,0:T(8,128)(2,1)}, /*index=5*/s32[]{:T(128)}, s32[]{:T(128)}, s32[]{:T(128)}, s32[]{:T(128)}) while((s32[]{:T(128)}, f32[24,64,128]{2,1,0:T(8,128)S(1)}, s32[]{:T(128)}, bf16[8,24]{1,0:T(8,128)(2,1)S(1)}, ...), condition=%wide.region_7.8_spmd, body=%wide.region_6.7_spmd.sunk | while | flops 589854 | bytes 1966475 | solution.py:52
  609.5 1.4 convolution_bitcast_fusion.2
  613.5 1.6 broadcast_multiply_fusion
  615.4 1.6 collective-permute-start.1
  617.2 4.2 collective-permute-done.1
  621.5 2.5 fusion.16
  (128 shorter events, 36.5 us)
Async XLA Ops:
  7.2 244.5 %copy-start = (bf16[1,128,768]{2,1,0:T(8,128)(2,1)S(1)}, bf16[1,128,768]{2,1,0:T(8,128)(2,1)}, u32[]{:S(2)}) copy-start(bf16[1,128,768]{2,1,0:T(8,128)(2,1)} %param.13) | copy-start | bytes 589828
  7.2 72.0 %all-gather.9.cloned.1.call-start = ((), (), s32[]{:S(2)}) async-start(), calls=%async_computation | async-start | bytes 5271552 | tf_op jit(solution)/shard_map/all_gather | solution.py:123
  7.9 180.0 %all-gather.13.cloned.1.call-start = ((), (), s32[]{:S(2)}) async-start(), calls=%async_computation.2 | async-start | bytes 7077888 | tf_op jit(solution)/shard_map/all_gather | solution.py:18
  9.0 77.0 %copy-start.19 = (f32[4,1792]{1,0:T(4,128)S(1)}, f32[4,1792]{1,0:T(4,128)}, u32[]{:S(2)}) copy-start(f32[4,1792]{1,0:T(4,128)} %param.17) | copy-start | bytes 86020
  82.6 6.6 %copy-start.5 = (bf16[128,3328]{1,0:T(8,128)(2,1)}, bf16[128,3328]{1,0:T(8,128)(2,1)S(1)}, u32[]{:S(2)}) copy-start(bf16[128,3328]{1,0:T(8,128)(2,1)S(1)} %convolution_convert_fusion) | copy-start | bytes 2555908
  82.7 4.8 collective-permute-start
  86.1 2.9 copy-start.11
  86.1 2.9 copy-start.13
  86.1 2.9 copy-start.15
  86.2 2.9 copy-start.17
  89.1 162.6 %copy-start.3 = (bf16[128,1792]{1,0:T(8,128)(2,1)}, bf16[128,1792]{1,0:T(8,128)(2,1)S(1)}, u32[]{:S(2)}) copy-start(bf16[128,1792]{1,0:T(8,128)(2,1)S(1)} %get-tuple-element.403) | copy-start | bytes 1376260
  89.5 2.2 copy-start.20
  90.8 160.9 %all-gather.11.cloned.1.call-start = ((), (), s32[]{:S(2)}) async-start(), calls=%async_computation.1 | async-start | bytes 2433024 | tf_op jit(solution)/shard_map/all_gather | solution.py:124
  91.5 437.7 %all-reduce.12.cloned.1.call-start = ((), (), s32[]{:S(2)}) async-start(), calls=%async_computation.4 | async-start | bytes 9437184
  197.3 54.4 %copy-start.18 = (f32[1536]{0:T(1024)S(1)}, f32[1536]{0:T(1024)}, u32[]{:S(2)}) copy-start(f32[1536]{0:T(1024)} %param.19) | copy-start | bytes 18436
  255.7 3.1 copy-start.1
  258.8 342.0 %all-gather.15.cloned.1.call-start = ((), (), s32[]{:S(2)}) async-start(), calls=%async_computation.3 | async-start | bytes 3538944 | tf_op jit(solution)/shard_map/all_gather | solution.py:35
  300.8 1.6 copy-start.10
  302.4 4.5 copy-start.2
  302.4 4.5 copy-start.8
  611.0 2.4 copy-start.4
  611.0 2.4 copy-start.6
  612.2 1.2 copy-start.7
  613.4 1.7 copy-start.12
  613.4 1.7 copy-start.14
  613.4 1.7 copy-start.16
  615.1 6.4 %slice-start = ((s8[5111808]{0:T(1024)(128)(4,1)}), s8[4194304]{0:T(1024)(128)(4,1)S(1)}, s32[]{:S(2)}) async-start(s8[5111808]{0:T(1024)(128)(4,1)} %bitcast.117), calls=%async_computation.5 | async-start | bytes 8388608
  615.3 6.2 slice-start.1
  615.4 6.2 copy-start.9
  615.4 6.0 collective-permute-start.1
Sparse Core Ops, SparseCore 0:
  9.8 69.3 all-gather.8
  90.9 96.9 all-gather.12
  189.8 61.8 all-gather.10
  258.9 270.3 all-reduce.11
  531.7 68.9 all-gather.14
where the time goes:
time: 632 us; the launch traced here: 631 us
  waiting for transfers between devices  487 us (77%)
  blocking collectives  47.3 us (7%)
  matrix products  33.2 us (5%)
  other arithmetic  29.1 us (5%)
  between operations  14.3 us (2%)
  local copies, waits for them, and re-layouts  14.2 us (2%)
    unnamed x6, waiting for transfers between devices  223 us
    all_gather x1, waiting for transfers between devices, shards(): lax.all_gather(in_w, 'stream', axis=0, tiled=True)  70.2 us
    all_gather x1, waiting for transfers between devices, carried_in(): lax.all_gather(a.astype(kind), axis)  68.9 us
    all_gather x1, waiting for transfers between devices, entering(): pieces = jax.tree.map(lambda part: lax.all_gather(part, axis), value)  67.1 us
    all_gather x1, waiting for transfers between devices, shards(): lax.all_gather(out_w, 'stream', axis=0, tiled=True)  52.8 us
    all_gather x1, blocking collectives, entering(): pieces = jax.tree.map(lambda part: lax.all_gather(part, axis), value)  24.1 us
    all_gather x1, blocking collectives, carried_in(): lax.all_gather(a.astype(kind), axis)  23.2 us
  transfers between devices with their start and end apart: 7, of which 7 were waited for; matrix products, arithmetic and copies ran while one was open for 7% of the time, Pallas kernels for 0%

commit v1 on v0

--- a/solution.py
+++ b/solution.py
@@ -121,7 +121,9 @@
     head_count = dskip.shape[0]
     full_in, full_out = (
         lax.all_gather(in_w, "stream", axis=0, tiled=True),
-        lax.all_gather(out_w, "stream", axis=0, tiled=True),
+        jnp.concatenate(
+            lax.all_to_all(jnp.stack([out_w] * lax.axis_size("stream")), "stream", 0, 0), axis=0
+        ),
     )
     inner_width = full_out.shape[0]
     proj_width = full_in.shape[1]

time: 632 us -> 592 us (0.937)
  waiting for transfers between devices: 487 us -> 436 us
  starting transfers between devices: 5.12 us -> 12.7 us
    all_gather x1 -> x0, waiting for transfers between devices: 52.8 us -> none  [shards(): lax.all_gather(out_w, 'stream', axis=0, tiled=True)]
    all_to_all x0 -> x1, starting transfers between devices: none -> 7.66 us  [shards(): lax.all_to_all(jnp.stack([out_w] * lax.axis_size('stream')), 'stream', 0, 0)]
    unnamed x6 -> x5, waiting for transfers between devices: 223 us -> 221 us
  transfers between devices with their start and end apart: 7 -> 7, of which waited for: 7 -> 6; matrix products, arithmetic and copies ran while one was open for 7% -> 8% of each run, Pallas kernels for 0% -> 0%
where the time goes in v1:
time: 592 us; the launch traced here: 590 us
  waiting for transfers between devices  436 us (74%)
  blocking collectives  45.1 us (8%)
  matrix products  34.9 us (6%)
  other arithmetic  30 us (5%)
  local copies, waits for them, and re-layouts  17.1 us (3%)
  between operations  14.3 us (2%)
  starting transfers between devices  12.7 us (2%)
    unnamed x5, waiting for transfers between devices  221 us
    all_gather x1, waiting for transfers between devices, shards(): lax.all_gather(in_w, 'stream', axis=0, tiled=True)  70.2 us
    all_gather x1, waiting for transfers between devices, entering(): pieces = jax.tree.map(lambda part: lax.all_gather(part, axis), value)  70.1 us
    all_gather x1, waiting for transfers between devices, carried_in(): lax.all_gather(a.astype(kind), axis)  68.9 us
    all_gather x1, blocking collectives, entering(): pieces = jax.tree.map(lambda part: lax.all_gather(part, axis), value)  24 us
    all_gather x1, blocking collectives, carried_in(): lax.all_gather(a.astype(kind), axis)  21.1 us
  transfers between devices with their start and end apart: 7, of which 6 were waited for; matrix products, arithmetic and copies ran while one was open for 8% of the time, Pallas kernels for 0%

profile of v1, /device:TPU:32, one launch (start us, length us, event | category | flops | bytes accessed | tf_op | source)
XLA Modules:
  0.0 590.3 jit_solution(8418887914674219678)
XLA Ops:
  9.0 70.2 %all-gather.8.cloned.1.call-done = bf16[768,3328]{1,0:T(8,128)(2,1)} async-done(((bf16[24,3328]{1,0:T(8,128)(2,1)}), bf16[768,3328]{1,0:T(8,128)(2,1)}) %all-gather.8.cloned.1.call-update) | async-done | bytes 5111824 | tf_op jit(solution)/shard_map/all_gather | solution.py:123
  79.2 3.4 convolution_convert_fusion
  82.7 3.4 collective-permute-start
  87.5 1.5 multiply_convert_fusion
  92.8 1.7 stack.2
  94.5 7.7 %all-to-all-start = ((bf16[32,48,768]{2,1,0:T(8,128)(2,1)}), bf16[32,48,768]{2,1,0:T(8,128)(2,1)}, u32[]{:S(2)}, u32[]{:S(2)}) async-start(bf16[32,48,768]{2,1,0:T(8,128)(2,1)} %stack.2), calls=%async_computation | async-start | bytes 4718592 | tf_op jit(solution)/shard_map/all_to_all | solution.py:125
  102.5 24.0 %all-gather.2 = f32[8,1,24]{2,1,0:T(1,128)S(1)} all-gather(f32[1,1,24]{2,1,0:T(1,128)S(1)} %get-tuple-element.413), channel_id=1, replica_groups=mesh['tm'=8,'stream'=32] {'tm'}, dimensions={0}, use_global_device_ids=true | all-gather | bytes 864 | tf_op jit(solution)/shard_map/all_gather | solution.py:18
  127.5 2.3 fusion.7
  131.4 70.1 %all-gather.10.cloned.1.call-done = f32[192,64,128]{2,1,0:T(8,128)} async-done(((f32[24,64,128]{2,1,0:T(8,128)}), f32[192,64,128]{2,1,0:T(8,128)}) %all-gather.10.cloned.1.call-update) | async-done | bytes 6291472 | tf_op jit(solution)/shard_map/all_gather | solution.py:18
  201.5 9.4 %while.21 = (s32[]{:T(128)}, f32[24,64,128]{2,1,0:T(8,128)S(1)}, s32[]{:T(128)}, f32[8,24]{1,0:T(8,128)S(1)}, f32[8,24,64,128]{3,2,1,0:T(8,128)}, /*index=5*/s32[]{:T(128)}, s32[]{:T(128)}) while((s32[]{:T(128)}, f32[24,64,128]{2,1,0:T(8,128)S(1)}, s32[]{:T(128)}, f32[8,24]{1,0:T(8,128)S(1)}, f32[8,24,64,128]{3,2,1,0:T(8,128)}, ...), condition=%wide.region_2.3_spmd.clone, body=%wide.region_1.2_spmd.clone.sunk | while | flops 786436 | bytes 2359697 | solution.py:27
  212.5 4.0 multiply_reduce_fusion
  216.5 3.0 convolution_bitcast_fusion
  219.6 3.5 broadcast_multiply_fusion.4
  223.4 1.9 convolution_convert_fusion.1
  225.3 21.1 %all-gather.3 = bf16[8,1,24]{2,1,0:T(2,128)(2,1)S(1)} all-gather(bf16[1,1,24]{2,1,0:T(2,128)(2,1)S(1)} %get-tuple-element.411), channel_id=1, replica_groups=mesh['tm'=8,'stream'=32] {'tm'}, dimensions={0}, use_global_device_ids=true | all-gather | bytes 432 | tf_op jit(solution)/shard_map/all_gather | solution.py:35
  247.4 2.3 copy.57
  251.6 2.1 fusion.14
  253.6 2.3 copy.59
  256.0 2.1 mul.434
  258.1 1.4 copy.58
  262.5 1.6 convolution_add_fusion.1
  264.1 1.5 convolution_add_fusion.2
  265.6 2.9 fusion.15
  268.5 220.5 %all-reduce.12.cloned.1.call-done = f32[768,1536]{0,1:T(8,128)} async-done(((f32[768,1536]{0,1:T(8,128)}), f32[768,1536]{0,1:T(8,128)}) %all-reduce.12.cloned.1.call-update) | async-done | bytes 4718608
  489.0 1.7 dynamic-slice_multiply_fusion
  491.6 68.9 %all-gather.12.cloned.1.call-done = bf16[192,64,128]{2,1,0:T(8,128)(2,1)} async-done(((bf16[24,64,128]{2,1,0:T(8,128)(2,1)}), bf16[192,64,128]{2,1,0:T(8,128)(2,1)}) %all-gather.12.cloned.1.call-update) | async-done | bytes 3145744 | tf_op jit(solution)/shard_map/all_gather | solution.py:35
  560.6 8.7 %while.20 = (s32[]{:T(128)}, f32[24,64,128]{2,1,0:T(8,128)S(1)}, s32[]{:T(128)}, bf16[8,24]{1,0:T(8,128)(2,1)S(1)}, bf16[8,24,64,128]{3,2,1,0:T(8,128)(2,1)}, /*index=5*/s32[]{:T(128)}, s32[]{:T(128)}, s32[]{:T(128)}, s32[]{:T(128)}) while((s32[]{:T(128)}, f32[24,64,128]{2,1,0:T(8,128)S(1)}, s32[]{:T(128)}, bf16[8,24]{1,0:T(8,128)(2,1)S(1)}, ...), condition=%wide.region_7.8_spmd, body=%wide.region_6.7_spmd.sunk | while | flops 589854 | bytes 1966475 | solution.py:52
  569.3 1.4 convolution_bitcast_fusion.2
  573.2 1.6 broadcast_multiply_fusion
  575.2 1.6 collective-permute-start.1
  577.0 4.2 collective-permute-done.1
  581.3 2.5 fusion.16
  (128 shorter events, 39.3 us)
Async XLA Ops:
  7.2 205.3 %copy-start = (bf16[1,128,768]{2,1,0:T(8,128)(2,1)S(1)}, bf16[1,128,768]{2,1,0:T(8,128)(2,1)}, u32[]{:S(2)}) copy-start(bf16[1,128,768]{2,1,0:T(8,128)(2,1)} %param.13) | copy-start | bytes 589828
  7.2 72.0 %all-gather.8.cloned.1.call-start = ((), (), s32[]{:S(2)}) async-start(), calls=%async_computation.1 | async-start | bytes 5271552 | tf_op jit(solution)/shard_map/all_gather | solution.py:123
  7.9 193.6 %all-gather.10.cloned.1.call-start = ((), (), s32[]{:S(2)}) async-start(), calls=%async_computation.2 | async-start | bytes 7077888 | tf_op jit(solution)/shard_map/all_gather | solution.py:18
  9.0 77.0 %copy-start.19 = (f32[4,1792]{1,0:T(4,128)S(1)}, f32[4,1792]{1,0:T(4,128)}, u32[]{:S(2)}) copy-start(f32[4,1792]{1,0:T(4,128)} %param.17) | copy-start | bytes 86020
  82.6 8.9 %copy-start.5 = (bf16[128,3328]{1,0:T(8,128)(2,1)}, bf16[128,3328]{1,0:T(8,128)(2,1)S(1)}, u32[]{:S(2)}) copy-start(bf16[128,3328]{1,0:T(8,128)(2,1)S(1)} %convolution_convert_fusion) | copy-start | bytes 2555908
  82.7 4.8 collective-permute-start
  86.1 2.9 copy-start.10
  86.1 2.9 copy-start.12
  86.1 2.9 copy-start.14
  86.2 2.9 copy-start.16
  89.1 123.4 %copy-start.3 = (bf16[128,1792]{1,0:T(8,128)(2,1)}, bf16[128,1792]{1,0:T(8,128)(2,1)S(1)}, u32[]{:S(2)}) copy-start(bf16[128,1792]{1,0:T(8,128)(2,1)S(1)} %get-tuple-element.403) | copy-start | bytes 1376260
  91.5 1.3 copy-start.17
  94.5 7.9 %copy-start.20 = (f32[24]{0:T(128)S(1)}, f32[24]{0:T(128)}, u32[]{:S(2)}) copy-start(f32[24]{0:T(128)} %param.18) | copy-start | bytes 292
  94.5 117.9 %all-to-all-start = ((bf16[32,48,768]{2,1,0:T(8,128)(2,1)}), bf16[32,48,768]{2,1,0:T(8,128)(2,1)}, u32[]{:S(2)}, u32[]{:S(2)}) async-start(bf16[32,48,768]{2,1,0:T(8,128)(2,1)} %stack.2), calls=%async_computation | async-start | bytes 4718592 | tf_op jit(solution)/shard_map/all_to_all | solution.py:125
  102.2 386.8 %all-reduce.12.cloned.1.call-start = ((), (), s32[]{:S(2)}) async-start(), calls=%async_computation.4 | async-start | bytes 9437184
  210.9 1.6 copy-start.18
  216.5 3.1 copy-start.1
  219.5 341.0 %all-gather.12.cloned.1.call-start = ((), (), s32[]{:S(2)}) async-start(), calls=%async_computation.3 | async-start | bytes 3538944 | tf_op jit(solution)/shard_map/all_gather | solution.py:35
  259.5 1.6 copy-start.9
  261.1 4.5 copy-start.2
  570.7 2.5 copy-start.4
  570.7 2.5 copy-start.6
  572.0 1.2 copy-start.7
  573.2 1.7 copy-start.11
  573.2 1.7 copy-start.13
  573.2 1.7 copy-start.15
  574.9 6.4 %slice-start = ((s8[5111808]{0:T(1024)(128)(4,1)}), s8[4194304]{0:T(1024)(128)(4,1)S(1)}, s32[]{:S(2)}) async-start(s8[5111808]{0:T(1024)(128)(4,1)} %bitcast.118), calls=%async_computation.5 | async-start | bytes 8388608
  575.1 6.2 %slice-start.1 = ((s8[5111808]{0:T(1024)(128)(4,1)}), s8[917504]{0:T(1024)(128)(4,1)S(1)}, s32[]{:S(2)}) async-start(s8[5111808]{0:T(1024)(128)(4,1)} %bitcast.118), calls=%async_computation.6 | async-start | bytes 1835008
  575.1 6.2 %copy-start.8 = (bf16[128,1536]{1,0:T(8,128)(2,1)S(1)}, bf16[128,1536]{1,0:T(8,128)(2,1)}, u32[]{:S(2)}) copy-start(bf16[128,1536]{1,0:T(8,128)(2,1)} %get-tuple-element.405) | copy-start | bytes 1179652
  575.2 6.0 %collective-permute-start.1 = (f32[3,1792]{1,0:T(4,128)S(1)}, f32[3,1792]{1,0:T(4,128)S(1)}, u32[]{:S(2)}, u32[]{:S(2)}) collective-permute-start(f32[3,1792]{1,0:T(4,128)S(1)} %pad_add_fusion.1), channel_id=1, source_target_pairs={{32,0},{64,32},{96,64},{128,96},{160,128},{192,160},{224,192},{33,... | collective-permute-start | bytes 64520 | tf_op jit(solution)/shard_map/ppermute | solution.py:13
Sparse Core Ops, SparseCore 0:
  9.8 69.3 all-gather.7
  93.0 108.4 all-gather.9
  219.6 269.3 all-reduce.11
  491.5 68.9 all-gather.11
